TPU v7x, 32 devices: a whole 2x2x4 slice. The times are simulated.
32 devices in a mesh: dom: 2 (over y), feat: 4 (over z), dp: 4 (over x, core).
Axes of the slice: x: 2, y: 2, z: 4, core: 2. Of those that a mesh axis runs over, the one named last changes fastest.
Arguments:
- layer_in: bfloat16 [32768, 2048], P(('dom', 'dp', 'feat')), parts along dimension 0, may hold values from -6 to 6
- grad_out: bfloat16 [32768, 2048], P(('dom', 'dp', 'feat')), parts along dimension 0, may hold values from -6 to 6
- in_proj: bfloat16 [2048, 256], replicated, may hold values from -0.125 to 0.125
- out_proj: bfloat16 [2048, 256], replicated, may hold values from -0.125 to 0.125
- queries: bfloat16 [2048, 65536], P(('dom', 'dp'), 'feat'), parts along dimension 0, may hold values from -0.00390625 to 0.00390625
- seq_ids: int32 [32, 1024], P(('dom', 'dp', 'feat')), parts along dimension 0, may hold values from 0 to 15, never falling along the last dimension, each value on 1 to 128 neighbouring positions
- valid_counts: int32 [512], P(('dom', 'dp', 'feat')), parts along dimension 0, may hold values from 16 to 128
- owner_order: int32 [2048], P(('dom', 'dp')), parts along dimension 0, may hold values from 0 to 1023, as said below
Outputs:
- scores: float32 [2048, 256], P(('dom', 'dp', 'feat')), parts along dimension 0
There are 2 independent parts, one for each index of `dom`. A program takes and returns all parts, laid end to end along the dimension named above; an argument that names none is the same for every part. Nothing has to cross between parts.
Inputs may be any that keep to these rules, and one draw needn't show every extreme that they name: `seq_ids`: each row numbers the 16 sequences of one block in order, never falling; every number appears. `owner_order`: within each aligned block of 256 rows, a permutation of that block's row numbers.
All inputs are finite; a program needn't handle non-finite values.
Results may differ from a plain program's by a relative error of at most 0.005.
Values may be sent and summed in bfloat16 or wider, within the bound.
A program may use at most 64 MiB of HBM per device.

v0:
```python
import jax
import jax.numpy as jnp
from jax import lax
from jax.sharding import PartitionSpec as P

WIN = 128


def local(layer_in, grad_out, in_proj, out_proj, queries, seq_ids, valid_counts, owner_order):
    in_low = jnp.dot(layer_in, in_proj, preferred_element_type=jnp.float32).astype(jnp.bfloat16)
    out_low = jnp.dot(grad_out, out_proj, preferred_element_type=jnp.float32).astype(jnp.bfloat16)
    proj_width = in_proj.shape[1]
    seq_count = valid_counts.shape[0]
    labels = seq_ids[0]
    member = (labels[:, None] == jnp.arange(seq_count, dtype=jnp.int32)[None, :]).astype(jnp.int32)
    seg_len = jnp.sum(member, axis=0)
    starts = jnp.cumsum(seg_len) - seg_len
    keep_len = jnp.minimum(seg_len, valid_counts)
    padding = jnp.zeros((WIN, proj_width), jnp.bfloat16)
    in_pad = jnp.concatenate([in_low, padding], axis=0)
    out_pad = jnp.concatenate([out_low, padding], axis=0)

    def windows(first_row):
        return (
            lax.dynamic_slice_in_dim(in_pad, first_row, WIN, 0),
            lax.dynamic_slice_in_dim(out_pad, first_row, WIN, 0),
        )

    in_win, out_win = jax.vmap(windows)(starts)
    usable = jnp.arange(WIN, dtype=jnp.int32)[None, :] < keep_len[:, None]
    in_win = jnp.where(usable[:, :, None], in_win, jnp.zeros((), jnp.bfloat16))
    seq_grads = jnp.einsum("swi,swj->sij", in_win, out_win, preferred_element_type=jnp.float32)
    seq_grads = seq_grads.astype(jnp.bfloat16).reshape(seq_count, proj_width * proj_width)
    train_rows = lax.all_to_all(seq_grads, "feat", split_axis=1, concat_axis=0, tiled=True)
    query_rows = queries.shape[0]
    ordered = jnp.take(queries, owner_order % query_rows, axis=0)
    scored = lax.dot_general(
        ordered,
        lax.all_gather(train_rows, "dp", axis=0, tiled=True),
        (((1,), (1,)), ((), ())),
        preferred_element_type=jnp.float32,
    )
    result = lax.psum_scatter(scored, "feat", scatter_dimension=0, tiled=True)
    return result


def solution(mesh):
    in_specs = (
        P(("dom", "dp", "feat"), None),
        P(("dom", "dp", "feat"), None),
        P(),
        P(),
        P(("dom", "dp"), "feat"),
        P(("dom", "dp", "feat"), None),
        P(("dom", "dp", "feat")),
        P(("dom", "dp")),
    )
    out_specs = P(("dom", "dp", "feat"), None)
    return jax.shard_map(local, mesh=mesh, in_specs=in_specs, out_specs=out_specs, check_vma=False)
```

profile of v0, /device:TPU:0, one launch (start us, length us, event | category | flops | bytes accessed | tf_op | source)
XLA Modules:
  0.0 214.1 jit_solution(496399708918642620)
XLA Ops:
  6.5 0.9 convert_reduce_fusion
  7.4 0.7 min.3
  8.4 3.4 %convolution_convert_fusion.1 = bf16[1024,256]{1,0:T(8,128)(2,1)S(1)} fusion(bf16[1024,2048]{1,0:T(8,128)(2,1)} %param.9, bf16[2048,256]{1,0:T(8,128)(2,1)S(1)} %copy-done), kind=kOutput, calls=%fused_computation.10 | convolution fusion | flops 1074003968 | bytes 5767168 | tf_op jit(solution)/shard_map/dot_general | solution.py:11
  12.0 20.2 %while.3 = (s32[]{:T(128)}, bf16[1152,256]{1,0:T(8,128)(2,1)S(1)}, s32[16,2]{0,1:T(2,128)S(1)}, bf16[16,128,256]{2,1,0:T(8,128)(2,1)S(1)}, s32[]{:T(128)}) while((s32[]{:T(128)}, bf16[1152,256]{1,0:T(8,128)(2,1)S(1)}, s32[16,2]{0,1:T(2,128)S(1)}, bf16[16,128,256]{2,1,0:T(8,128)(2,1)S(1)}, s32[]{:T(128)}) %tuple.34), condition=%wide.while_cond.1, body=%wide.while_body.1.sunk | while | flops 2 | bytes 131177 | solution.py:26
  12.6 0.6 bitcast_dynamic-update-slice_fusion.5
  32.2 4.1 %convolution_convert_fusion.2 = bf16[1024,256]{1,0:T(8,128)(2,1)S(1)} fusion(bf16[1024,2048]{1,0:T(8,128)(2,1)} %param.8, bf16[2048,256]{1,0:T(8,128)(2,1)} %param.10), kind=kOutput, calls=%fused_computation.11 | convolution fusion | flops 1074003968 | bytes 5767168 | tf_op jit(solution)/shard_map/dot_general | solution.py:10
  36.5 20.5 %while.2 = (s32[]{:T(128)}, bf16[1152,256]{1,0:T(8,128)(2,1)S(1)}, s32[16,2]{0,1:T(2,128)S(1)}, bf16[16,128,256]{2,1,0:T(8,128)(2,1)S(1)}, s32[]{:T(128)}) while((s32[]{:T(128)}, bf16[1152,256]{1,0:T(8,128)(2,1)S(1)}, s32[16,2]{0,1:T(2,128)S(1)}, bf16[16,128,256]{2,1,0:T(8,128)(2,1)S(1)}, s32[]{:T(128)}) %tuple.44), condition=%wide.while_cond, body=%wide.while_body.sunk | while | flops 2 | bytes 131177 | solution.py:25
  37.1 0.7 bitcast_dynamic-update-slice_fusion.4
  38.4 0.7 bitcast_dynamic-update-slice_fusion.4
  39.6 0.7 bitcast_dynamic-update-slice_fusion.4
  40.9 0.7 bitcast_dynamic-update-slice_fusion.4
  42.2 0.7 bitcast_dynamic-update-slice_fusion.4
  43.5 0.7 bitcast_dynamic-update-slice_fusion.4
  44.8 0.7 bitcast_dynamic-update-slice_fusion.4
  46.0 0.7 bitcast_dynamic-update-slice_fusion.4
  47.3 0.7 bitcast_dynamic-update-slice_fusion.4
  48.6 0.7 bitcast_dynamic-update-slice_fusion.4
  49.9 0.7 bitcast_dynamic-update-slice_fusion.4
  51.2 0.7 bitcast_dynamic-update-slice_fusion.4
  52.4 0.7 bitcast_dynamic-update-slice_fusion.4
  53.7 0.7 bitcast_dynamic-update-slice_fusion.4
  55.0 0.7 bitcast_dynamic-update-slice_fusion.4
  56.3 0.7 bitcast_dynamic-update-slice_fusion.4
  57.0 1.0 copy-done.1
  58.0 2.7 %convolution_convert_fusion = bf16[16,256,256]{2,1,0:T(8,128)(2,1)S(1)} fusion(bf16[16,128,256]{2,1,0:T(8,128)(2,1)} %copy-done.2, bf16[16,128,256]{2,1,0:T(8,128)(2,1)} %copy-done.1, pred[16,128]{1,0:T(8,128)(4,1)S(1)} %iota_compare_fusion.1), kind=kOutput, calls=%fused_computation.9 | convolution fusion | flops 270008320 | bytes 4196352 | tf_op jit(solution)/shard_map/swi,swj->sij/dot_general | solution.py:32
  60.6 2.8 %all_to_all.14 = bf16[16,4,16384]{2,1,0:T(4,128)(2,1)} reshape(bf16[16,256,256]{2,1,0:T(8,128)(2,1)S(1)} %convolution_convert_fusion) | data formatting | bytes 4194304 | tf_op jit(solution)/shard_map/all_to_all | solution.py:34
  63.4 2.7 %copy.25 = bf16[16,4,16384]{2,0,1:T(8,128)(2,1)S(1)} copy(bf16[16,4,16384]{2,1,0:T(4,128)(2,1)} %all_to_all.14) | data formatting | bytes 4194304 | tf_op jit(solution)/shard_map/all_to_all | solution.py:34
  66.1 54.4 %all_to_all.19 = bf16[16,4,16384]{2,0,1:T(8,128)(2,1)} all-to-all(bf16[16,4,16384]{2,0,1:T(8,128)(2,1)S(1)} %copy.25), channel_id=1, replica_groups=mesh['dom'=2,'feat'=4,'dp'=4] {'feat'}, dimensions={1} | all-to-all | bytes 4194304 | tf_op jit(solution)/shard_map/all_to_all | solution.py:34
  120.9 21.0 %gather_fusion = bf16[256,16384]{1,0:T(8,128)(2,1)} fusion(bf16[256,16384]{1,0:T(8,128)(2,1)} %param.12, s32[1024]{0:T(1024)S(1)} %pad_clamp_fusion), kind=kCustom, calls=%fused_computation | custom fusion | bytes 16778240 | tf_op jit(solution)/shard_map/jit(_take)/gather | solution.py:36
  141.9 36.4 %all-gather.2.cloned.1.call-done = bf16[256,16384]{1,0:T(8,128)(2,1)} async-done(((bf16[64,16384]{1,0:T(8,128)(2,1)}), bf16[256,16384]{1,0:T(8,128)(2,1)}) %all-gather.2.cloned.1.call-update) | async-done | bytes 8388624 | tf_op jit(solution)/shard_map/all_gather | solution.py:39
  178.3 8.8 %fusion = f32[256,256]{1,0:T(8,128)} fusion(bf16[256,16384]{1,0:T(8,128)(2,1)} %all-gather.2.cloned.1.call-done, bf16[256,16384]{1,0:T(8,128)(2,1)} %gather_fusion, pred[256]{0:T(512)(128)(4,1)S(1)} %get-tuple-element.61), kind=kOutput, calls=%fused_computation.5 | convolution fusion | flops 2151677952 | bytes 17039616 | tf_op jit(solution)/shard_map/dot_general | solution.py:37
  187.1 20.1 %reduce-scatter.2.cloned.1.call-done = f32[64,256]{1,0:T(8,128)} async-done(((f32[256,256]{1,0:T(8,128)}), f32[64,256]{1,0:T(8,128)}) %reduce-scatter.2.cloned.1.call-update) | async-done | bytes 65552 | tf_op jit(solution)/shard_map/reduce_scatter | solution.py:43
  (102 shorter events, 29.4 us)
Async XLA Ops:
  6.5 1.9 copy-start
  6.5 171.7 %all-gather.2.cloned.1.call-start = ((), (), s32[]{:S(2)}) async-start(), calls=%async_computation.2 | async-start | bytes 10485760 | tf_op jit(solution)/shard_map/all_gather | solution.py:39
  32.2 4.1 %copy-start.2 = (bf16[16,128,256]{2,1,0:T(8,128)(2,1)}, bf16[16,128,256]{2,1,0:T(8,128)(2,1)S(1)}, u32[]{:S(2)}) copy-start(bf16[16,128,256]{2,1,0:T(8,128)(2,1)S(1)} %get-tuple-element.20) | copy-start | bytes 3145732
  57.0 1.0 copy-start.1
  60.6 60.2 %copy-start.3 = (s32[256]{0:T(256)S(1)}, s32[256]{0:T(256)}, u32[]{:S(2)}) copy-start(s32[256]{0:T(256)} %param.15) | copy-start | bytes 3076
  120.6 86.7 %reduce-scatter.2.cloned.1.call-start = ((), (), s32[]{:S(2)}) async-start(), calls=%async_computation.3 | async-start | bytes 327680 | tf_op jit(solution)/shard_map/reduce_scatter | solution.py:43
Sparse Core Ops, SparseCore 0:
  120.7 57.4 all-gather.1
  187.3 19.9 reduce-scatter.1
where the time goes:
time: 215 us; the launch traced here: 214 us
  local copies, waits for them, and re-layouts  67.9 us (32%)
  waiting for transfers between devices  56.5 us (26%)
  blocking collectives  54.4 us (25%)
  matrix products  19 us (9%)
  between operations  13.5 us (6%)
    all_to_all x1, blocking collectives, local(): lax.all_to_all(seq_grads, 'feat', split_axis=1, concat_axis=0, tiled=True)  54.4 us
    gather x96, local copies, waits for them, and re-layouts  39.9 us
    all_gather x1, waiting for transfers between devices, local(): lax.all_gather(train_rows, 'dp', axis=0, tiled=True)  36.4 us
    gather x1, local copies, waits for them, and re-layouts, local(): ordered = jnp.take(queries, owner_order % query_rows, axis=0)  21 us
    reduce_scatter x1, waiting for transfers between devices, local(): result = lax.psum_scatter(scored, 'feat', scatter_dimension=0, tiled=True)  20.1 us
    dot_general x1, matrix products, local(): lax.dot_general(ordered, lax.all_gather(train_rows, 'dp', axis=0, tiled=T...  8.83 us
    all_to_all x2, local copies, waits for them, and re-layouts, local(): lax.all_to_all(seq_grads, 'feat', split_axis=1, concat_axis=0, tiled=True)  5.5 us
  transfers between devices with their start and end apart: 2, of which 2 were waited for; matrix products, arithmetic and copies ran while one was open for 10% of the time, Pallas kernels for 0%

commit v1 on v0

v1 whole, which is shorter than its diff:
```python
import functools

import jax
import jax.numpy as jnp
from jax import lax
from jax.experimental import pallas as pl
from jax.experimental.pallas import tpu as pltpu
from jax.sharding import PartitionSpec as P

MESH = pl.DeviceIdType.MESH
F32 = jnp.float32
BF16 = jnp.bfloat16


def grads_kernel(steps, tile, x_ref, g_ref, wi_ref, wo_ref, ids_ref, cnt_ref, out_ref, in_t, out_low):
    step = pl.program_id(0)
    at = pl.ds(pl.multiple_of(step * tile, tile), tile)
    low = jnp.dot(x_ref[...], wi_ref[...], preferred_element_type=F32)
    in_t[:, at] = low.astype(BF16).astype(F32).T
    out_low[at, :] = jnp.dot(g_ref[...], wo_ref[...], preferred_element_type=F32).astype(BF16)

    @pl.when(step == steps - 1)
    def _():
        width, seqs, _ = out_ref.shape
        tokens = in_t.shape[1]
        labels = ids_ref[...]
        rows = lax.broadcasted_iota(jnp.int32, (seqs, tokens), 0)
        cols = lax.broadcasted_iota(jnp.int32, (seqs, tokens), 1)
        starts = jnp.sum((labels < rows).astype(F32), axis=1, keepdims=True).astype(jnp.int32)
        mask = ((labels == rows) & (cols - starts < cnt_ref[...])).astype(F32)
        some = 16

        def body(k, carry):
            span = pl.ds(pl.multiple_of(k * some, some), some)
            left = in_t[span, :][:, None, :] * mask[None, :, :]
            left = left.reshape(some * seqs, tokens).astype(BF16)
            got = jnp.dot(left, out_low[...], preferred_element_type=F32)
            out_ref[span] = got.astype(BF16).reshape(some, seqs, width)
            return carry

        lax.fori_loop(0, width // some, body, 0)


def seq_grads_of(layer_in, grad_out, in_proj, out_proj, seq_ids, valid_counts):
    tokens, model = layer_in.shape
    width = in_proj.shape[1]
    seqs = valid_counts.shape[0]
    tile = min(256, tokens)
    steps = tokens // tile
    return pl.pallas_call(
        functools.partial(grads_kernel, steps, tile),
        grid=(steps,),
        out_shape=jax.ShapeDtypeStruct((width, seqs, width), BF16),
        in_specs=[
            pl.BlockSpec((tile, model), lambda i: (i, 0)),
            pl.BlockSpec((tile, model), lambda i: (i, 0)),
            pl.BlockSpec((model, width), lambda i: (0, 0)),
            pl.BlockSpec((model, width), lambda i: (0, 0)),
            pl.BlockSpec((1, tokens), lambda i: (0, 0)),
            pl.BlockSpec((seqs, 1), lambda i: (0, 0)),
        ],
        out_specs=pl.BlockSpec((width, seqs, width), lambda i: (0, 0, 0)),
        scratch_shapes=[pltpu.VMEM((width, tokens), F32), pltpu.VMEM((tokens, width), BF16)],
        compiler_params=pltpu.CompilerParams(vmem_limit_bytes=48 * 1024 * 1024),
    )(layer_in, grad_out, in_proj, out_proj, seq_ids, valid_counts.reshape(seqs, 1))


def flip(i, m):
    bit = 1
    while bit <= m:
        if m & bit:
            i = i + bit - 2 * bit * (lax.div(i, bit) % 2)
        bit *= 2
    return i


def score_kernel(fn, dn, chunks, grads, queries, order, out, held, q_buf, acc, perm, piece, landed,
                 q_sem, own_sem, a_send, a_recv, d_send, d_recv, r_send, r_recv):
    me_f = lax.axis_index("feat")
    me_d = lax.axis_index("dp")
    slab = held.shape[2]
    seqs = held.shape[3]
    width = held.shape[4]
    q_rows = queries.shape[0]
    rows = q_rows // fn
    part = slab // chunks
    bits = []
    bit = dn // 2
    while bit >= 1:
        bits.append(bit)
        bit //= 2

    barrier = pltpu.get_barrier_semaphore()
    for r in range(1, fn):
        pl.semaphore_signal(barrier, inc=1, device_id={"feat": flip(me_f, r)}, device_id_type=MESH)
    for b in bits:
        pl.semaphore_signal(barrier, inc=1, device_id={"dp": flip(me_d, b)}, device_id_type=MESH)
    pl.semaphore_wait(barrier, fn - 1 + len(bits))

    def across(r, c):
        other = flip(me_f, r)
        return pltpu.make_async_remote_copy(
            src_ref=grads.at[pl.ds(other * slab + c * part, part)],
            dst_ref=held.at[me_f, me_d, pl.ds(c * part, part)],
            send_sem=a_send.at[r, c],
            recv_sem=a_recv.at[r, c],
            device_id={"feat": other},
            device_id_type=MESH,
        )

    def own(c):
        return pltpu.make_async_copy(
            grads.at[pl.ds(me_f * slab + c * part, part)],
            held.at[me_f, me_d, pl.ds(c * part, part)],
            own_sem.at[c],
        )

    def along(r, m, b, c):
        block = held.at[flip(me_f, r), flip(me_d, m), pl.ds(c * part, part)]
        return pltpu.make_async_remote_copy(
            src_ref=block,
            dst_ref=block,
            send_sem=d_send.at[r, m + b, c],
            recv_sem=d_recv.at[r, m + b, c],
            device_id={"dp": flip(me_d, b)},
            device_id_type=MESH,
        )

    q_copy = pltpu.make_async_copy(queries, q_buf, q_sem)
    for c in range(chunks):
        own(c).start()
    for r in range(1, fn):
        for c in range(chunks):
            across(r, c).start()
    q_copy.start()

    at_row = lax.broadcasted_iota(jnp.int32, (q_rows, q_rows), 0)
    perm[...] = ((order[...] % q_rows) == at_row).astype(F32).T

    def masks_before(k):
        got = [0]
        for b in bits[:k]:
            got = got + [m + b for m in got]
        return got

    def stage(k, r, c):
        if k == 0:
            if r == 0:
                own(c).wait()
            else:
                across(r, c).wait_recv()
        else:
            for m in masks_before(k - 1):
                along(r, m, bits[k - 1], c).wait_recv()
        if k < len(bits):
            for m in masks_before(k):
                along(r, m, bits[k], c).start()

    def score(r, c):
        source = flip(me_f, r)

        def body(i, total):
            left = q_buf[:, pl.ds(pl.multiple_of(i * width, width), width)]
            right = held[source, :, i].reshape(dn * seqs, width)
            return total + lax.dot_general(left, right, (((1,), (1,)), ((), ())), preferred_element_type=F32)

        start = jnp.zeros(acc.shape, F32) if c == 0 else acc[...]
        acc[...] = lax.fori_loop(c * part, (c + 1) * part, body, start)
        if c == chunks - 1:
            ordered = jnp.dot(perm[...], acc[...], precision=lax.Precision.HIGHEST, preferred_element_type=F32)
            piece[:, source] = ordered.reshape(fn, rows, dn * seqs)

            def send(t, carry):
                other = lax.rem(me_f + t, fn)
                pltpu.make_async_remote_copy(
                    src_ref=piece.at[other, source],
                    dst_ref=landed.at[me_f, source],
                    send_sem=r_send.at[other],
                    recv_sem=r_recv.at[me_f],
                    device_id={"feat": other},
                    device_id_type=MESH,
                ).start()
                return carry

            lax.fori_loop(1, fn, send, 0)

    events = [(r, c) for r in range(fn) for c in range(chunks)]
    last = len(bits)
    for e in range(len(events) + last):
        for k in range(last + 1):
            if 0 <= e - k < len(events):
                stage(k, *events[e - k])
        if e - last == 0:
            q_copy.wait()
        if e >= last:
            score(*events[e - last])

    total = piece[me_f]
    for r in range(1, fn):
        other = flip(me_f, r)
        pltpu.make_async_copy(landed.at[other], landed.at[other], r_recv.at[other]).wait()
        total = total + landed[other]
    out[...] = total
    for r in range(1, fn):
        other = flip(me_f, r)
        pltpu.make_async_copy(piece.at[other], piece.at[other], r_send.at[other]).wait()
        for c in range(chunks):
            across(r, c).wait_send()
    for r, c in events:
        for k, b in enumerate(bits):
            for m in masks_before(k):
                along(r, m, b, c).wait_send()


def scores_of(fn, dn, grads, queries, owner_order):
    width, seqs, _ = grads.shape
    q_rows, feats = queries.shape
    slab = width // fn
    rows = q_rows // fn
    chunks = max(1, min(4, slab // 16))
    dma = pltpu.SemaphoreType.DMA
    return pl.pallas_call(
        functools.partial(score_kernel, fn, dn, chunks),
        out_shape=jax.ShapeDtypeStruct((fn, rows, dn * seqs), F32),
        in_specs=[
            pl.BlockSpec(memory_space=pl.ANY),
            pl.BlockSpec(memory_space=pl.ANY),
            pl.BlockSpec(memory_space=pltpu.VMEM),
        ],
        out_specs=pl.BlockSpec(memory_space=pltpu.VMEM),
        scratch_shapes=[
            pltpu.VMEM((fn, dn, slab, seqs, width), BF16),
            pltpu.VMEM((q_rows, feats), BF16),
            pltpu.VMEM((q_rows, dn * seqs), F32),
            pltpu.VMEM((q_rows, q_rows), F32),
            pltpu.VMEM((fn, fn, rows, dn * seqs), F32),
            pltpu.VMEM((fn, fn, rows, dn * seqs), F32),
            dma,
            dma((chunks,)),
            dma((fn, chunks)),
            dma((fn, chunks)),
            dma((fn, dn, chunks)),
            dma((fn, dn, chunks)),
            dma((fn,)),
            dma((fn,)),
        ],
        compiler_params=pltpu.CompilerParams(
            collective_id=0, has_side_effects=True, vmem_limit_bytes=56 * 1024 * 1024
        ),
    )(grads, queries, owner_order.reshape(1, q_rows))


def local(fn, dn, layer_in, grad_out, in_proj, out_proj, queries, seq_ids, valid_counts, owner_order):
    grads = seq_grads_of(layer_in, grad_out, in_proj, out_proj, seq_ids, valid_counts)
    got = scores_of(fn, dn, grads, queries, owner_order)
    rows = got.shape[1]
    seqs = valid_counts.shape[0]
    return got.reshape(fn, rows, dn, seqs).transpose(1, 2, 0, 3).reshape(rows, dn * fn * seqs)


def solution(mesh):
    in_specs = (
        P(("dom", "dp", "feat"), None),
        P(("dom", "dp", "feat"), None),
        P(),
        P(),
        P(("dom", "dp"), "feat"),
        P(("dom", "dp", "feat"), None),
        P(("dom", "dp", "feat")),
        P(("dom", "dp")),
    )
    out_specs = P(("dom", "dp", "feat"), None)
    body = functools.partial(local, mesh.shape["feat"], mesh.shape["dp"])
    return jax.shard_map(body, mesh=mesh, in_specs=in_specs, out_specs=out_specs, check_vma=False)
```

time: 215 us -> 98.4 us (0.46)
  Pallas kernels: 0 us -> 91.1 us
  local copies, waits for them, and re-layouts: 67.9 us -> 6.91 us
  waiting for transfers between devices: 56.5 us -> 0 us
  blocking collectives: 54.4 us -> 0 us
  matrix products: 19 us -> 0 us
  between operations: 13.5 us -> 0.04 us
    pallas_call x0 -> x2, Pallas kernels: none -> 91.1 us  [the longest x1 80.5 us: scores_of(): pl.pallas_call(functools.partial(score_kernel, fn, dn, chunks), out_shape...]
    gather x97 -> x0, local copies, waits for them, and re-layouts: 60.9 us -> none
    all_to_all x1 -> x0, blocking collectives: 54.4 us -> none  [local(): lax.all_to_all(seq_grads, 'feat', split_axis=1, concat_axis=0, tiled=True)]
    all_gather x1 -> x0, waiting for transfers between devices: 36.4 us -> none  [local(): lax.all_gather(train_rows, 'dp', axis=0, tiled=True)]
    reduce_scatter x1 -> x0, waiting for transfers between devices: 20.1 us -> none  [local(): result = lax.psum_scatter(scored, 'feat', scatter_dimension=0, tiled=True)]
    dot_general x4 -> x0, matrix products: 19 us -> none  [the longest x1 8.83 us: local(): lax.dot_general(ordered, lax.all_gather(train_rows, 'dp', axis=0, tiled=T...]
    all_to_all x2 -> x0, local copies, waits for them, and re-layouts: 5.5 us -> none  [local(): lax.all_to_all(seq_grads, 'feat', split_axis=1, concat_axis=0, tiled=True)]
    unnamed x11 -> x8, local copies, waits for them, and re-layouts: 1.29 us -> 4.46 us
  transfers between devices with their start and end apart: 2 -> 0, of which waited for: 2 -> 0; matrix products, arithmetic and copies ran while one was open for 10% -> 0% of each run, Pallas kernels for 0% -> 0%
where the time goes in v1:
time: 98.4 us; the launch traced here: 98.1 us
  Pallas kernels  91.1 us (93%)
  local copies, waits for them, and re-layouts  6.91 us (7%)
    pallas_call x1, Pallas kernels, scores_of(): pl.pallas_call(functools.partial(score_kernel, fn, dn, chunks), out_shape...  80.5 us
    pallas_call x1, Pallas kernels, seq_grads_of(): pl.pallas_call(functools.partial(grads_kernel, steps, tile), grid=(steps,...  10.6 us
    unnamed x8, local copies, waits for them, and re-layouts  4.46 us

profile of v1, /device:TPU:0, one launch (start us, length us, event | category | flops | bytes accessed | tf_op | source)
XLA Modules:
  0.0 98.1 jit_solution(1545689210051787787)
XLA Ops:
  0.0 0.7 copy.11.cnt_ref
  0.7 0.0 copy-start.1
  0.7 1.2 %copy-done.1 = bf16[2048,256]{1,0:T(8,128)(2,1)S(1)} copy-done((bf16[2048,256]{1,0:T(8,128)(2,1)S(1)}, bf16[2048,256]{1,0:T(8,128)(2,1)}, u32[]{:S(2)}) %copy-start.1) | copy-done | bytes 1048600
  2.0 0.0 copy-start.2
  2.0 1.2 %copy-done.2 = bf16[2048,256]{1,0:T(8,128)(2,1)S(1)} copy-done((bf16[2048,256]{1,0:T(8,128)(2,1)S(1)}, bf16[2048,256]{1,0:T(8,128)(2,1)}, u32[]{:S(2)}) %copy-start.2) | copy-done | bytes 1048600
  3.2 0.0 copy-start.3
  3.2 0.7 copy-done.3
  3.9 10.6 %shard_map.82.grads = bf16[256,16,256]{2,1,0:T(8,128)(2,1)S(1)} custom-call(bf16[1024,2048]{1,0:T(8,128)(2,1)} %x_ref.1, bf16[1024,2048]{1,0:T(8,128)(2,1)} %g_ref.1, bf16[2048,256]{1,0:T(8,128)(2,1)S(1)} %copy-done.1, bf16[2048,256]{1,0:T(8,128)(2,1)S(1)} %copy-done.2, s32[1,1024]{1,0:T(1,128)S(1)} %copy-done.3, s32[16,1]{1,0:T(8,128)S(1)} %copy.11.cnt_ref), custom_call_target="tpu_custom_call" | custom-call | tf_op jit(solution)/shard_map/pallas_call | solution.py:50
  14.5 0.0 copy-start
  14.5 1.3 %copy-done = bf16[256,16,256]{2,1,0:T(8,128)(2,1)} copy-done((bf16[256,16,256]{2,1,0:T(8,128)(2,1)}, bf16[256,16,256]{2,1,0:T(8,128)(2,1)S(1)}, u32[]{:S(2)}) %copy-start) | copy-done | bytes 2097176
  15.8 80.5 %shard_map.83 = f32[4,64,64]{2,1,0:T(8,128)} custom-call(bf16[256,16,256]{2,1,0:T(8,128)(2,1)} %copy-done, bf16[256,16384]{1,0:T(8,128)(2,1)} %queries.1, s32[1,256]{1,0:T(1,128)} %bitcast.8), custom_call_target="tpu_custom_call" | custom-call | tf_op jit(solution)/shard_map/pallas_call | solution.py:222
  96.3 1.0 %copy.12 = f32[4,64,64]{1,2,0:T(8,128)S(1)} copy(f32[4,64,64]{2,1,0:T(8,128)} %shard_map.83) | data formatting | bytes 131072 | tf_op jit(solution)/shard_map/pallas_call | solution.py:222
  97.4 0.7 copy.14
  (1 shorter events, 0.0 us)
Async XLA Ops:
  0.7 1.2 %copy-start.1 = (bf16[2048,256]{1,0:T(8,128)(2,1)S(1)}, bf16[2048,256]{1,0:T(8,128)(2,1)}, u32[]{:S(2)}) copy-start(bf16[2048,256]{1,0:T(8,128)(2,1)} %wi_ref.1) | copy-start | bytes 3145732
  2.0 1.2 %copy-start.2 = (bf16[2048,256]{1,0:T(8,128)(2,1)S(1)}, bf16[2048,256]{1,0:T(8,128)(2,1)}, u32[]{:S(2)}) copy-start(bf16[2048,256]{1,0:T(8,128)(2,1)} %wo_ref.1) | copy-start | bytes 3145732
  3.2 0.7 copy-start.3
  14.5 1.3 %copy-start = (bf16[256,16,256]{2,1,0:T(8,128)(2,1)}, bf16[256,16,256]{2,1,0:T(8,128)(2,1)S(1)}, u32[]{:S(2)}) copy-start(bf16[256,16,256]{2,1,0:T(8,128)(2,1)S(1)} %shard_map.82.grads) | copy-start | bytes 6291460

commit v2 on v1

--- a/solution.py
+++ b/solution.py
@@ -27,7 +27,11 @@
         rows = lax.broadcasted_iota(jnp.int32, (seqs, tokens), 0)
         cols = lax.broadcasted_iota(jnp.int32, (seqs, tokens), 1)
         starts = jnp.sum((labels < rows).astype(F32), axis=1, keepdims=True).astype(jnp.int32)
-        mask = ((labels == rows) & (cols - starts < cnt_ref[...])).astype(F32)
+        one_r = lax.broadcasted_iota(jnp.int32, (seqs, seqs), 0)
+        one_c = lax.broadcasted_iota(jnp.int32, (seqs, seqs), 1)
+        counts = jnp.where(one_r == one_c, cnt_ref[...].astype(F32), 0.0)
+        counts = jnp.sum(counts, axis=1, keepdims=True).astype(jnp.int32)
+        mask = ((labels == rows) & (cols - starts < counts)).astype(F32)
         some = 16
 
         def body(k, carry):
@@ -57,12 +61,12 @@
             pl.BlockSpec((model, width), lambda i: (0, 0)),
             pl.BlockSpec((model, width), lambda i: (0, 0)),
             pl.BlockSpec((1, tokens), lambda i: (0, 0)),
-            pl.BlockSpec((seqs, 1), lambda i: (0, 0)),
+            pl.BlockSpec((1, seqs), lambda i: (0, 0)),
         ],
         out_specs=pl.BlockSpec((width, seqs, width), lambda i: (0, 0, 0)),
         scratch_shapes=[pltpu.VMEM((width, tokens), F32), pltpu.VMEM((tokens, width), BF16)],
-        compiler_params=pltpu.CompilerParams(vmem_limit_bytes=48 * 1024 * 1024),
-    )(layer_in, grad_out, in_proj, out_proj, seq_ids, valid_counts.reshape(seqs, 1))
+        compiler_params=pltpu.CompilerParams(vmem_limit_bytes=67043328),
+    )(layer_in, grad_out, in_proj, out_proj, seq_ids, valid_counts.reshape(1, seqs))
 
 
 def flip(i, m):
@@ -159,13 +163,12 @@
     def score(r, c):
         source = flip(me_f, r)
 
-        def body(i, total):
-            left = q_buf[:, pl.ds(pl.multiple_of(i * width, width), width)]
-            right = held[source, :, i].reshape(dn * seqs, width)
-            return total + lax.dot_general(left, right, (((1,), (1,)), ((), ())), preferred_element_type=F32)
-
-        start = jnp.zeros(acc.shape, F32) if c == 0 else acc[...]
-        acc[...] = lax.fori_loop(c * part, (c + 1) * part, body, start)
+        blocks = [held[source, :, c * part + i].reshape(dn * seqs, width) for i in range(part)]
+        span = slice(c * part * width, (c + 1) * part * width)
+        got = lax.dot_general(
+            q_buf[:, span], jnp.concatenate(blocks, axis=1), (((1,), (1,)), ((), ())), preferred_element_type=F32
+        )
+        acc[...] = got if c == 0 else acc[...] + got
         if c == chunks - 1:
             ordered = jnp.dot(perm[...], acc[...], precision=lax.Precision.HIGHEST, preferred_element_type=F32)
             piece[:, source] = ordered.reshape(fn, rows, dn * seqs)
@@ -245,7 +248,7 @@
             dma((fn,)),
         ],
         compiler_params=pltpu.CompilerParams(
-            collective_id=0, has_side_effects=True, vmem_limit_bytes=56 * 1024 * 1024
+            collective_id=0, has_side_effects=True, vmem_limit_bytes=67043328
         ),
     )(grads, queries, owner_order.reshape(1, q_rows))
 

time: 98.4 us -> 84 us (0.85)
  Pallas kernels: 91.1 us -> 82.1 us
  local copies, waits for them, and re-layouts: 6.91 us -> 1.72 us
    pallas_call x1, Pallas kernels: 80.5 us -> 69.5 us  [scores_of(): pl.pallas_call(functools.partial(score_kernel, fn, dn, chunks), out_shape...]
    unnamed x8 -> x0, local copies, waits for them, and re-layouts: 4.46 us -> none
    pallas_call x1, Pallas kernels: 10.6 us -> 12.6 us  [seq_grads_of(): pl.pallas_call(functools.partial(grads_kernel, steps, tile), grid=(steps,...]
where the time goes in v2:
time: 84 us; the launch traced here: 83.9 us
  Pallas kernels  82.1 us (98%)
  local copies, waits for them, and re-layouts  1.72 us (2%)
    pallas_call x1, Pallas kernels, scores_of(): pl.pallas_call(functools.partial(score_kernel, fn, dn, chunks), out_shape...  69.5 us
    pallas_call x1, Pallas kernels, seq_grads_of(): pl.pallas_call(functools.partial(grads_kernel, steps, tile), grid=(steps,...  12.6 us

profile of v2, /device:TPU:0, one launch (start us, length us, event | category | flops | bytes accessed | tf_op | source)
XLA Modules:
  0.0 83.9 jit_solution(13598818914523420539)
XLA Ops:
  0.0 12.6 %shard_map.82.grads = bf16[256,16,256]{2,1,0:T(8,128)(2,1)} custom-call(bf16[1024,2048]{1,0:T(8,128)(2,1)} %x_ref.1, bf16[1024,2048]{1,0:T(8,128)(2,1)} %g_ref.1, bf16[2048,256]{1,0:T(8,128)(2,1)} %wi_ref.1, bf16[2048,256]{1,0:T(8,128)(2,1)} %wo_ref.1, s32[1,1024]{1,0:T(1,128)} %ids_ref.1, s32[1,16]{1,0:T(1,128)} %bitcast.9), custom_call_target="tpu_custom_call" | custom-call | tf_op jit(solution)/shard_map/pallas_call | solution.py:54
  12.6 69.5 %shard_map.83 = f32[4,64,64]{2,1,0:T(8,128)} custom-call(bf16[256,16,256]{2,1,0:T(8,128)(2,1)} %shard_map.82.grads, bf16[256,16384]{1,0:T(8,128)(2,1)} %queries.1, s32[1,256]{1,0:T(1,128)} %bitcast.8), custom_call_target="tpu_custom_call" | custom-call | tf_op jit(solution)/shard_map/pallas_call | solution.py:225
  82.1 1.0 %copy.10 = f32[4,64,64]{1,2,0:T(8,128)S(1)} copy(f32[4,64,64]{2,1,0:T(8,128)} %shard_map.83) | data formatting | bytes 131072 | tf_op jit(solution)/shard_map/pallas_call | solution.py:225
  83.1 0.7 copy.12
  (1 shorter events, 0.0 us)

commit v3 on v2

--- a/solution.py
+++ b/solution.py
@@ -42,7 +42,7 @@
             out_ref[span] = got.astype(BF16).reshape(some, seqs, width)
             return carry
 
-        lax.fori_loop(0, width // some, body, 0)
+        lax.fori_loop(0, width // some, body, 0, unroll=2)
 
 
 def seq_grads_of(layer_in, grad_out, in_proj, out_proj, seq_ids, valid_counts):
@@ -220,7 +220,7 @@
     q_rows, feats = queries.shape
     slab = width // fn
     rows = q_rows // fn
-    chunks = max(1, min(4, slab // 16))
+    chunks = max(1, min(8, slab // 8))
     dma = pltpu.SemaphoreType.DMA
     return pl.pallas_call(
         functools.partial(score_kernel, fn, dn, chunks),

time: 84 us -> 93.2 us (1.11)
  Pallas kernels: 82.1 us -> 91.2 us
    pallas_call x1, Pallas kernels: 69.5 us -> 80 us  [scores_of(): pl.pallas_call(functools.partial(score_kernel, fn, dn, chunks), out_shape...]
    pallas_call x1, Pallas kernels: 12.6 us -> 11.2 us  [seq_grads_of(): pl.pallas_call(functools.partial(grads_kernel, steps, tile), grid=(steps,...]
where the time goes in v3:
time: 93.2 us; the launch traced here: 93 us
  Pallas kernels  91.2 us (98%)
  local copies, waits for them, and re-layouts  1.72 us (2%)
    pallas_call x1, Pallas kernels, scores_of(): pl.pallas_call(functools.partial(score_kernel, fn, dn, chunks), out_shape...  80 us
    pallas_call x1, Pallas kernels, seq_grads_of(): pl.pallas_call(functools.partial(grads_kernel, steps, tile), grid=(steps,...  11.2 us

profile of v3, /device:TPU:0, one launch (start us, length us, event | category | flops | bytes accessed | tf_op | source)
XLA Modules:
  0.0 93.0 jit_solution(1674294172740212461)
XLA Ops:
  0.0 11.2 %shard_map.82.grads = bf16[256,16,256]{2,1,0:T(8,128)(2,1)} custom-call(bf16[1024,2048]{1,0:T(8,128)(2,1)} %x_ref.1, bf16[1024,2048]{1,0:T(8,128)(2,1)} %g_ref.1, bf16[2048,256]{1,0:T(8,128)(2,1)} %wi_ref.1, bf16[2048,256]{1,0:T(8,128)(2,1)} %wo_ref.1, s32[1,1024]{1,0:T(1,128)} %ids_ref.1, s32[1,16]{1,0:T(1,128)} %bitcast.9), custom_call_target="tpu_custom_call" | custom-call | tf_op jit(solution)/shard_map/pallas_call | solution.py:54
  11.2 80.0 %shard_map.83 = f32[4,64,64]{2,1,0:T(8,128)} custom-call(bf16[256,16,256]{2,1,0:T(8,128)(2,1)} %shard_map.82.grads, bf16[256,16384]{1,0:T(8,128)(2,1)} %queries.1, s32[1,256]{1,0:T(1,128)} %bitcast.8), custom_call_target="tpu_custom_call" | custom-call | tf_op jit(solution)/shard_map/pallas_call | solution.py:225
  91.2 1.0 %copy.10 = f32[4,64,64]{1,2,0:T(8,128)S(1)} copy(f32[4,64,64]{2,1,0:T(8,128)} %shard_map.83) | data formatting | bytes 131072 | tf_op jit(solution)/shard_map/pallas_call | solution.py:225
  92.3 0.7 copy.12
  (1 shorter events, 0.0 us)
